TPU v7x, 32 devices: a whole 2x2x4 slice. The times are simulated.
32 devices in a mesh: group: 8 (over y, x, core), member: 4 (over z).
Axes of the slice: x: 2, y: 2, z: 4, core: 2. Of those that a mesh axis runs over, the one named last changes fastest.
Arguments:
- tokens: bfloat16 [4096, 2048], P(('group', 'member')), may hold values from -6 to 6
- grad_out: bfloat16 [4096, 2048], P(('group', 'member')), may hold values from -6 to 6
- expert_ids: int32 [4096, 8], P(('group', 'member')), may hold values from 0 to 31, as said below
- pair_slot: int32 [4096, 8], P(('group', 'member')), may hold values from 0 to 47, as said below
- gate_weights: bfloat16 [4096, 8], P(('group', 'member')), may hold values from 0.049804688 to 1
- weight_gate: bfloat16 [32, 2048, 768], P(('group', 'member')), may hold values from -0.125 to 0.125
- weight_up: bfloat16 [32, 2048, 768], P(('group', 'member')), may hold values from -0.125 to 0.125
- weight_down: bfloat16 [32, 768, 2048], P(('group', 'member')), may hold values from -0.21875 to 0.21875
- saved_gate: bfloat16 [32, 1536, 768], P(('group', 'member')), may hold values from -6 to 6
- saved_up: bfloat16 [32, 1536, 768], P(('group', 'member')), may hold values from -6 to 6
Outputs:
- grad_tokens: bfloat16 [4096, 2048], P(('group', 'member'))
- grad_gates: bfloat16 [4096, 8], P(('group', 'member'))
- grad_weight_gate: bfloat16 [32, 2048, 768], P(('group', 'member'))
- grad_weight_up: bfloat16 [32, 2048, 768], P(('group', 'member'))
- grad_weight_down: bfloat16 [32, 768, 2048], P(('group', 'member'))
Inputs may be any that keep to these rules, and one draw needn't show every extreme that they name: `expert_ids`: each token names 8 distinct experts, two in each of exactly 4 groups, the group of expert e being e // 4. The tokens of one device send at most 96 tokens to one group, and in every draw some group gets exactly 96 from every device. `pair_slot`: among one device's assignments to one expert the slots are distinct and run from 0 to their count less one, in no fixed order of tokens. In every draw some expert gets exactly 48 assignments from every device.
All inputs are finite; a program needn't handle non-finite values.
Results may differ from a plain program's by a relative error of at most 0.012.
Values may be sent and summed in bfloat16 or wider, within the bound.
A program may use at most 192 MiB of HBM per device.

v0:
```python
import jax
import jax.numpy as jnp
from jax import lax
from jax.sharding import PartitionSpec as P

AXES = ("group", "member")
OVER_ROWS = (((0,), (0,)), ((), ()))
OVER_FEATURES = (((1,), (1,)), ((), ()))


def expert_block(
    token_rows,
    grad_rows,
    route_gate,
    saved_pregate,
    saved_preup,
    weight_gate,
    weight_up,
    weight_down,
):
    pre_gate = saved_pregate.astype(jnp.float32)
    pre_up = saved_preup.astype(jnp.float32)
    gate_sigmoid = jax.nn.sigmoid(pre_gate)
    gate_swish = pre_gate * gate_sigmoid
    hidden = gate_swish * pre_up
    hidden_low = hidden.astype(jnp.bfloat16)
    route_scale = route_gate.astype(jnp.float32)[:, None]
    scaled_grads = (route_scale * grad_rows.astype(jnp.float32)).astype(jnp.bfloat16)
    over_rows = (((0,), (0,)), ((), ()))
    over_features = (((1,), (1,)), ((), ()))
    down_grad = lax.dot_general(
        hidden_low, scaled_grads, over_rows, preferred_element_type=jnp.float32
    )
    back_hidden = lax.dot_general(
        grad_rows, weight_down, over_features, preferred_element_type=jnp.float32
    )
    slot_gate = jnp.sum(hidden * back_hidden, axis=1).astype(jnp.bfloat16)
    hidden_grad = route_scale * back_hidden
    pregate_grad = (
        hidden_grad * pre_up * gate_sigmoid * (1.0 + pre_gate * (1.0 - gate_sigmoid))
    ).astype(jnp.bfloat16)
    preup_grad = (hidden_grad * gate_swish).astype(jnp.bfloat16)
    gate_grad = lax.dot_general(
        token_rows, pregate_grad, over_rows, preferred_element_type=jnp.float32
    )
    up_grad = lax.dot_general(token_rows, preup_grad, over_rows, preferred_element_type=jnp.float32)
    slot_grad = (
        lax.dot_general(
            pregate_grad, weight_gate, over_features, preferred_element_type=jnp.float32
        )
        + lax.dot_general(preup_grad, weight_up, over_features, preferred_element_type=jnp.float32)
    ).astype(jnp.bfloat16)
    return (slot_grad, slot_gate, gate_grad, up_grad, down_grad)


def pair_body(
    tokens,
    grad_out,
    expert_ids,
    pair_slot,
    gate_weights,
    weight_gate,
    weight_up,
    weight_down,
    saved_gate,
    saved_up,
):
    groups = lax.axis_size("group")
    members = lax.axis_size("member")
    experts = groups * members
    tok_rows, model_width = tokens.shape
    route_count = expert_ids.shape[1]
    capacity = saved_gate.shape[1]
    pair_rows = capacity // experts
    token_range = jnp.arange(tok_rows, dtype=jnp.int32)
    dest = (expert_ids * pair_rows + pair_slot).reshape(-1)
    slot_token = (
        jnp.full((experts * pair_rows,), tok_rows, jnp.int32)
        .at[dest]
        .set(jnp.repeat(token_range, route_count))
    )
    send_rows = jnp.take(tokens, slot_token, axis=0, mode="fill", fill_value=0)
    send_grads = jnp.take(grad_out, slot_token, axis=0, mode="fill", fill_value=0)
    send_gates = (
        jnp.zeros((experts * pair_rows,), jnp.bfloat16).at[dest].set(gate_weights.reshape(-1))
    )
    expert_rows, expert_grads, expert_gates = (
        lax.all_to_all(send_rows, ("group", "member"), split_axis=0, concat_axis=0, tiled=True),
        lax.all_to_all(send_grads, ("group", "member"), split_axis=0, concat_axis=0, tiled=True),
        lax.all_to_all(send_gates, ("group", "member"), split_axis=0, concat_axis=0, tiled=True),
    )
    slot_grad, slot_gate, gate_total, up_total, down_total = expert_block(
        expert_rows,
        expert_grads,
        expert_gates,
        saved_gate[0],
        saved_up[0],
        weight_gate[0],
        weight_up[0],
        weight_down[0],
    )
    back_rows, back_terms = (
        lax.all_to_all(slot_grad, ("group", "member"), split_axis=0, concat_axis=0, tiled=True),
        lax.all_to_all(slot_gate, ("group", "member"), split_axis=0, concat_axis=0, tiled=True),
    )
    per_route = jnp.take(back_rows, dest, axis=0).reshape(tok_rows, route_count, model_width)
    grad_tokens = jnp.sum(per_route.astype(jnp.float32), axis=1).astype(jnp.bfloat16)
    grad_gates = jnp.take(back_terms, dest, axis=0).reshape(tok_rows, route_count)
    return (
        grad_tokens,
        grad_gates,
        gate_total[None].astype(jnp.bfloat16),
        up_total[None].astype(jnp.bfloat16),
        down_total[None].astype(jnp.bfloat16),
    )


def dense_body(
    tokens,
    grad_out,
    expert_ids,
    pair_slot,
    gate_weights,
    weight_gate,
    weight_up,
    weight_down,
    saved_gate,
    saved_up,
):
    groups = lax.axis_size("group")
    members = lax.axis_size("member")
    experts = groups * members
    me = lax.axis_index("group") * members + lax.axis_index("member")
    tok_rows, width = tokens.shape
    capacity = saved_gate.shape[1]
    pair = capacity // experts
    f32, bf16 = (jnp.float32, jnp.bfloat16)
    all_grads = lax.all_gather(grad_out, AXES, axis=0, tiled=True)
    meta = jnp.concatenate([expert_ids.astype(bf16), pair_slot.astype(bf16), gate_weights], axis=1)
    all_meta = lax.all_gather(meta, AXES, axis=0, tiled=True)
    route = expert_ids.shape[1]
    all_meta = all_meta.reshape(experts, tok_rows, 3, route).astype(f32)
    mine = all_meta[:, :, 0] == me.astype(f32)
    slot = jnp.sum(jnp.where(mine, all_meta[:, :, 1] + 1.0, 0.0), axis=2) - 1.0
    gate = jnp.sum(jnp.where(mine, all_meta[:, :, 2], 0.0), axis=2)
    pick = slot[:, None, :] == jnp.arange(pair, dtype=f32)[None, :, None]
    route_scale = jnp.sum(jnp.where(pick, gate[:, None, :], 0.0), axis=2).reshape(capacity, 1)
    pick = pick.astype(bf16)

    def rows_of(x):
        x = x.reshape(experts, tok_rows, width)
        got = lax.dot_general(pick, x, (((2,), (1,)), ((0,), (0,))), preferred_element_type=f32)
        return got.astype(bf16).reshape(capacity, width)

    grad_rows = rows_of(all_grads)
    all_tokens = lax.all_gather(tokens, AXES, axis=0, tiled=True)
    a = saved_gate[0].astype(f32)
    b = saved_up[0].astype(f32)
    sig = jax.nn.sigmoid(a)
    swish = a * sig
    hidden = swish * b
    back_hidden = lax.dot_general(
        grad_rows, weight_down[0], OVER_FEATURES, preferred_element_type=f32
    )
    slot_gate = jnp.sum(hidden * back_hidden, axis=1).astype(bf16)
    hidden_grad = route_scale * back_hidden
    pregate = (hidden_grad * b * sig * (1.0 + a * (1.0 - sig))).astype(bf16)
    preup = (hidden_grad * swish).astype(bf16)
    slot_grad = (
        lax.dot_general(pregate, weight_gate[0], OVER_FEATURES, preferred_element_type=f32)
        + lax.dot_general(preup, weight_up[0], OVER_FEATURES, preferred_element_type=f32)
    ).astype(bf16)
    back = lax.all_to_all(slot_grad, AXES, split_axis=0, concat_axis=0, tiled=True)
    terms = lax.all_to_all(slot_gate, AXES, split_axis=0, concat_axis=0, tiled=True)
    scaled = (route_scale * grad_rows.astype(f32)).astype(bf16)
    down_grad = lax.dot_general(hidden.astype(bf16), scaled, OVER_ROWS, preferred_element_type=f32)
    token_rows = rows_of(all_tokens)
    gate_grad = lax.dot_general(token_rows, pregate, OVER_ROWS, preferred_element_type=f32)
    up_grad = lax.dot_general(token_rows, preup, OVER_ROWS, preferred_element_type=f32)
    dest = expert_ids * pair + pair_slot
    hit = dest[:, :, None] == jnp.arange(capacity, dtype=jnp.int32)[None, None, :]
    grad_gates = jnp.sum(jnp.where(hit, terms.astype(f32), 0.0), axis=2).astype(bf16)
    grad_tokens = lax.dot_general(
        jnp.any(hit, axis=1).astype(bf16),
        back,
        (((1,), (0,)), ((), ())),
        preferred_element_type=f32,
    ).astype(bf16)
    return (
        grad_tokens,
        grad_gates,
        gate_grad.astype(bf16)[None],
        up_grad.astype(bf16)[None],
        down_grad.astype(bf16)[None],
    )


def body(*args):
    devices = lax.axis_size("group") * lax.axis_size("member")
    if devices * args[0].shape[0] <= 4 * args[8].shape[1]:
        return dense_body(*args)
    return pair_body(*args)


def solution(mesh):
    flat, deep = (P(AXES, None), P(AXES, None, None))
    return jax.shard_map(
        body,
        mesh=mesh,
        in_specs=(flat,) * 5 + (deep,) * 5,
        out_specs=(flat, flat, deep, deep, deep),
        check_vma=False,
    )
```

profile of v0, /device:TPU:8, one launch (start us, length us, event | category | flops | bytes accessed | tf_op | source)
XLA Modules:
  0.0 377.8 jit_solution(17915200260891188762)
XLA Ops:
  7.2 0.0 copy-start
  7.2 0.0 all-gather.3.cloned.1.call-start
  7.2 0.7 all-gather.3.cloned.1.call-update
  7.9 0.0 all-gather.5.cloned.1.call-start
  8.0 0.7 all-gather.5.cloned.1.call-update
  8.7 0.0 copy-start.6
  8.7 0.0 copy-start.7
  8.7 0.0 copy-start.8
  8.7 4.3 %copy.26 = bf16[1,1536,768]{1,2,0:T(8,128)(2,1)} copy(bf16[1,1536,768]{2,1,0:T(8,128)(2,1)} %param.19) | data formatting | bytes 4718592 | tf_op args[9]
  13.0 4.3 %copy.27 = bf16[1,1536,768]{1,2,0:T(8,128)(2,1)} copy(bf16[1,1536,768]{2,1,0:T(8,128)(2,1)} %param.18) | data formatting | bytes 4718592 | tf_op args[8]
  17.3 0.0 copy-done.6
  17.3 0.0 copy-done.7
  17.3 0.0 copy-done.8
  17.3 68.0 %all_gather.9 = bf16[4096,24]{0,1:T(8,128)(2,1)S(1)} all-gather(bf16[128,24]{0,1:T(8,128)(2,1)S(1)} %pad_maximum_fusion), channel_id=1, replica_groups=mesh['group'=8,'member'=4] {'group','member'}, dimensions={0}, use_global_device_ids=true | all-gather | bytes 202752 | tf_op jit(solution)/shard_map/all_gather | solution.py:140
  85.4 0.1 fusion.31
  85.5 0.3 select_reduce_fusion.1
  85.8 0.1 mul.61
  85.8 41.3 %all-gather.3.cloned.1.call-done = bf16[4096,2048]{1,0:T(8,128)(2,1)} async-done(((bf16[128,2048]{1,0:T(8,128)(2,1)}), bf16[4096,2048]{1,0:T(8,128)(2,1)}) %all-gather.3.cloned.1.call-update) | async-done | bytes 16777232 | tf_op jit(solution)/shard_map/all_gather | solution.py:138
  127.2 12.9 %multiply_convert_fusion = (bf16[32,48,2048]{2,1,0:T(8,128)(2,1)}, bf16[32,48,2048]{2,1,0:T(8,128)(2,1)}) fusion(f32[32,48]{1,0:T(8,128)S(1)} %select_reduce_fusion.1, bf16[32,128,2048]{2,1,0:T(8,128)(2,1)} %bitcast.84, f32[32,128]{1,0:T(8,128)S(1)} %broadcast_add_fusion), kind=kOutput, calls=%fused_computation | convolution fusion | flops 818085888 | bytes 29382656 | tf_op jit(solution)/shard_map/dot_general | solution.py:152
  140.1 0.0 copy-done.2
  140.1 11.7 %fusion.10 = (bf16[1536]{0:T(1024)(128)(2,1)S(1)}, bf16[1536,768]{0,1:T(8,128)(2,1)}, bf16[1536,768]{0,1:T(8,128)(2,1)}) fusion(bf16[1,1536,768]{1,2,0:T(8,128)(2,1)S(1)} %copy-done.2, bf16[1,1536,768]{1,2,0:T(8,128)(2,1)S(1)} %copy-done.4, f32[1536]{0:T(1024)S(1)} %mul.61, bf16[1536,2048]{1,0:T(8,128)(2,1)} %bitcast.89, bf16[1,768,2048]{2,1,0:T(8,128)(2,1)} %param.17), kind=kOutput, calls=%fused_computation.19 | convolution fusion | flops 4854249984 | bytes 18883584 | tf_op jit(solution)/shard_map/dot_general | solution.py:162
  151.8 0.7 convert_element_type.134
  152.5 4.0 %all-to-all-start.1 = ((bf16[32,48,1]{1,2,0:T(2,128)(2,1)}), bf16[32,48,1]{1,2,0:T(2,128)(2,1)S(1)}, u32[]{:S(2)}, u32[]{:S(2)}) async-start(bf16[32,48,1]{1,2,0:T(2,128)(2,1)} %convert_element_type.134), calls=%async_computation.1 | async-start | bytes 32768 | tf_op jit(solution)/shard_map/all_to_all | solution.py:174
  156.6 0.0 copy-start.9
  156.6 7.1 %fusion.20 = f32[1536,2048]{1,0:T(8,128)S(1)} fusion(bf16[1536,768]{0,1:T(8,128)(2,1)} %get-tuple-element.13, bf16[1,2048,768]{2,1,0:T(8,128)(2,1)S(1)} %copy-done), kind=kOutput, calls=%fused_computation.35 | convolution fusion | flops 4831838208 | bytes 18087936 | tf_op jit(solution)/shard_map/dot_general | solution.py:170
  163.7 0.0 copy-done.9
  163.7 0.0 copy-done.11
  163.7 7.5 %add_convert_fusion = bf16[1536,2048]{1,0:T(8,128)(2,1)} fusion(f32[1536,2048]{1,0:T(8,128)S(1)} %fusion.20, bf16[1536,768]{0,1:T(8,128)(2,1)S(1)} %copy-done.11, bf16[1,2048,768]{2,1,0:T(8,128)(2,1)S(1)} %copy-done.9), kind=kOutput, calls=%fused_computation.1 | convolution fusion | flops 4838129664 | bytes 24379392 | tf_op jit(solution)/shard_map/dot_general | solution.py:171
  171.2 0.0 all-to-all-done.1
  171.2 5.9 %all-to-all-start = ((bf16[32,48,2048]{2,1,0:T(8,128)(2,1)}), bf16[32,48,2048]{2,1,0:T(8,128)(2,1)}, u32[]{:S(2)}, u32[]{:S(2)}) async-start(bf16[32,48,2048]{2,1,0:T(8,128)(2,1)} %bitcast.92), calls=%async_computation | async-start | bytes 12582912 | tf_op jit(solution)/shard_map/all_to_all | solution.py:173
  177.1 0.1 copy.25
  177.2 3.1 fusion.3
  180.4 134.2 %all-gather.5.cloned.1.call-done = bf16[4096,2048]{1,0:T(8,128)(2,1)} async-done(((bf16[128,2048]{1,0:T(8,128)(2,1)}), bf16[4096,2048]{1,0:T(8,128)(2,1)}) %all-gather.5.cloned.1.call-update) | async-done | bytes 16777232 | tf_op jit(solution)/shard_map/all_gather | solution.py:156
  314.6 8.2 %convolution_convert_fusion = bf16[32,48,2048]{2,1,0:T(8,128)(2,1)S(1)} fusion(bf16[32,128,2048]{2,1,0:T(8,128)(2,1)} %bitcast.85, f32[32,128]{1,0:T(8,128)S(1)} %broadcast_add_fusion), kind=kOutput, calls=%fused_computation.29 | convolution fusion | flops 808648704 | bytes 23085056 | tf_op jit(solution)/shard_map/dot_general | solution.py:152
  322.8 0.0 copy-done.10
  322.9 0.0 copy-start.12
  322.9 0.0 slice-start
  322.9 6.5 %fusion.24 = bf16[1,2048,768]{2,1,0:T(8,128)(2,1)} fusion(bf16[1536,2048]{1,0:T(8,128)(2,1)S(1)} %bitcast.90, bf16[1536,768]{0,1:T(8,128)(2,1)S(1)} %copy-done.10), kind=kOutput, calls=%fused_computation.39 | convolution fusion | flops 4833411072 | bytes 11796480 | tf_op jit(solution)/shard_map/dot_general | solution.py:178
  329.4 6.5 %fusion.25 = bf16[1,2048,768]{2,1,0:T(8,128)(2,1)} fusion(bf16[1536,2048]{1,0:T(8,128)(2,1)S(1)} %bitcast.91, bf16[1536,768]{0,1:T(8,128)(2,1)S(1)} %copy-done.12), kind=kOutput, calls=%fused_computation.40 | convolution fusion | flops 4833411072 | bytes 11796480 | tf_op jit(solution)/shard_map/dot_general | solution.py:179
  336.0 0.0 copy-done.5
  336.0 0.0 copy-start.1
  336.0 7.2 %fusion.26 = bf16[1,768,2048]{2,1,0:T(8,128)(2,1)} fusion(bf16[1536,2048]{1,0:T(8,128)(2,1)S(1)} %bitcast.88, bf16[1,1536,768]{1,2,0:T(8,128)(2,1)S(1)} %copy-done.3, bf16[1,1536,768]{1,2,0:T(8,128)(2,1)S(1)} %copy-done.5), kind=kOutput, calls=%fused_computation.41 | convolution fusion | flops 4842848256 | bytes 14155776 | tf_op jit(solution)/shard_map/dot_general | solution.py:176
  343.2 0.1 convert_reduce_fusion
  343.2 0.1 reshape.75
  343.3 1.0 select_reduce_fusion
  344.2 0.7 copy.29
  344.9 21.5 %all-to-all-done = bf16[32,48,2048]{2,1,0:T(8,128)(2,1)} async-done(((bf16[32,48,2048]{2,1,0:T(8,128)(2,1)}), bf16[32,48,2048]{2,1,0:T(8,128)(2,1)}, u32[]{:S(2)}, u32[]{:S(2)}) %all-to-all-start) | async-done | bytes 6291488 | tf_op jit(solution)/shard_map/all_to_all | solution.py:173
  366.4 4.6 %convolution_convert_fusion.5 = bf16[128,2048]{1,0:T(8,128)(2,1)} fusion(pred[128,1536]{1,0:T(8,128)(4,1)S(1)} %fusion.3, bf16[1536,2048]{1,0:T(8,128)(2,1)} %bitcast.10), kind=kOutput, calls=%fused_computation.42 | convolution fusion | flops 805568512 | bytes 7012352 | tf_op jit(solution)/shard_map/dot_general | solution.py:183
  (19 shorter events, 0.1 us)
Async XLA Ops:
  7.2 149.4 %copy-start = (bf16[1,2048,768]{2,1,0:T(8,128)(2,1)S(1)}, bf16[1,2048,768]{2,1,0:T(8,128)(2,1)}, u32[]{:S(2)}) copy-start(bf16[1,2048,768]{2,1,0:T(8,128)(2,1)} %param.15) | copy-start | bytes 9437188
  7.2 120.0 %all-gather.3.cloned.1.call-start = ((), (), s32[]{:S(2)}) async-start(), calls=%async_computation.2 | async-start | bytes 17301504 | tf_op jit(solution)/shard_map/all_gather | solution.py:138
  7.9 306.7 %all-gather.5.cloned.1.call-start = ((), (), s32[]{:S(2)}) async-start(), calls=%async_computation.3 | async-start | bytes 17301504 | tf_op jit(solution)/shard_map/all_gather | solution.py:156
  8.7 8.6 %copy-start.6 = (s32[128,8]{0,1:T(8,128)S(1)}, s32[128,8]{0,1:T(8,128)}, u32[]{:S(2)}) copy-start(s32[128,8]{0,1:T(8,128)} %param.12) | copy-start | bytes 12292
  8.7 8.6 %copy-start.7 = (s32[128,8]{0,1:T(8,128)S(1)}, s32[128,8]{0,1:T(8,128)}, u32[]{:S(2)}) copy-start(s32[128,8]{0,1:T(8,128)} %param.13) | copy-start | bytes 12292
  8.7 8.6 %copy-start.8 = (bf16[128,8]{0,1:T(8,128)(2,1)S(1)}, bf16[128,8]{0,1:T(8,128)(2,1)}, u32[]{:S(2)}) copy-start(bf16[128,8]{0,1:T(8,128)(2,1)} %param.14) | copy-start | bytes 6148
  127.2 12.9 %copy-start.2 = (bf16[1,1536,768]{1,2,0:T(8,128)(2,1)S(1)}, bf16[1,1536,768]{1,2,0:T(8,128)(2,1)}, u32[]{:S(2)}) copy-start(bf16[1,1536,768]{1,2,0:T(8,128)(2,1)} %copy.26) | copy-start | bytes 7077892
  127.2 12.9 %copy-start.4 = (bf16[1,1536,768]{1,2,0:T(8,128)(2,1)S(1)}, bf16[1,1536,768]{1,2,0:T(8,128)(2,1)}, u32[]{:S(2)}) copy-start(bf16[1,1536,768]{1,2,0:T(8,128)(2,1)} %copy.27) | copy-start | bytes 7077892
  152.5 18.7 %all-to-all-start.1 = ((bf16[32,48,1]{1,2,0:T(2,128)(2,1)}), bf16[32,48,1]{1,2,0:T(2,128)(2,1)S(1)}, u32[]{:S(2)}, u32[]{:S(2)}) async-start(bf16[32,48,1]{1,2,0:T(2,128)(2,1)} %convert_element_type.134), calls=%async_computation.1 | async-start | bytes 32768 | tf_op jit(solution)/shard_map/all_to_all | solution.py:174
  156.6 7.1 %copy-start.9 = (bf16[1,2048,768]{2,1,0:T(8,128)(2,1)S(1)}, bf16[1,2048,768]{2,1,0:T(8,128)(2,1)}, u32[]{:S(2)}) copy-start(bf16[1,2048,768]{2,1,0:T(8,128)(2,1)} %param.16) | copy-start | bytes 9437188
  156.6 7.1 %copy-start.11 = (bf16[1536,768]{0,1:T(8,128)(2,1)S(1)}, bf16[1536,768]{0,1:T(8,128)(2,1)}, u32[]{:S(2)}) copy-start(bf16[1536,768]{0,1:T(8,128)(2,1)} %get-tuple-element.14) | copy-start | bytes 7077892
  171.2 195.2 %all-to-all-start = ((bf16[32,48,2048]{2,1,0:T(8,128)(2,1)}), bf16[32,48,2048]{2,1,0:T(8,128)(2,1)}, u32[]{:S(2)}, u32[]{:S(2)}) async-start(bf16[32,48,2048]{2,1,0:T(8,128)(2,1)} %bitcast.92), calls=%async_computation | async-start | bytes 12582912 | tf_op jit(solution)/shard_map/all_to_all | solution.py:173
  314.6 8.2 %copy-start.10 = (bf16[1536,768]{0,1:T(8,128)(2,1)S(1)}, bf16[1536,768]{0,1:T(8,128)(2,1)}, u32[]{:S(2)}) copy-start(bf16[1536,768]{0,1:T(8,128)(2,1)} %get-tuple-element.13) | copy-start | bytes 7077892
  322.9 6.6 %copy-start.12 = (bf16[1536,768]{0,1:T(8,128)(2,1)S(1)}, bf16[1536,768]{0,1:T(8,128)(2,1)}, u32[]{:S(2)}) copy-start(bf16[1536,768]{0,1:T(8,128)(2,1)} %get-tuple-element.14) | copy-start | bytes 7077892
  322.9 13.1 %slice-start = ((s8[6291456]{0:T(1024)(128)(4,1)}), s8[4194304]{0:T(1024)(128)(4,1)S(1)}, s32[]{:S(2)}) async-start(s8[6291456]{0:T(1024)(128)(4,1)} %bitcast.86), calls=%async_computation.4 | async-start | bytes 8388608
  329.4 6.5 %slice-start.1 = ((s8[6291456]{0:T(1024)(128)(4,1)}), s8[2097152]{0:T(1024)(128)(4,1)S(1)}, s32[]{:S(2)}) async-start(s8[6291456]{0:T(1024)(128)(4,1)} %bitcast.86), calls=%async_computation.5 | async-start | bytes 4194304
  329.4 6.5 %copy-start.3 = (bf16[1,1536,768]{1,2,0:T(8,128)(2,1)S(1)}, bf16[1,1536,768]{1,2,0:T(8,128)(2,1)}, u32[]{:S(2)}) copy-start(bf16[1,1536,768]{1,2,0:T(8,128)(2,1)} %copy.26) | copy-start | bytes 7077892
  329.4 6.5 %copy-start.5 = (bf16[1,1536,768]{1,2,0:T(8,128)(2,1)S(1)}, bf16[1,1536,768]{1,2,0:T(8,128)(2,1)}, u32[]{:S(2)}) copy-start(bf16[1,1536,768]{1,2,0:T(8,128)(2,1)} %copy.27) | copy-start | bytes 7077892
  336.0 35.0 %copy-start.1 = (bf16[1,2048,768]{2,1,0:T(8,128)(2,1)S(1)}, bf16[1,2048,768]{2,1,0:T(8,128)(2,1)}, u32[]{:S(2)}) copy-start(bf16[1,2048,768]{2,1,0:T(8,128)(2,1)} %param.15) | copy-start | bytes 9437188
Sparse Core Ops, SparseCore 0:
  11.0 116.1 all-gather.2
  130.2 184.4 all-gather.4
where the time goes:
time: 378 us
  waiting for transfers between devices  198 us (52%)
  matrix products  72.3 us (19%)
  blocking collectives  68 us (18%)
  between operations  14.3 us (4%)
  local copies, waits for them, and re-layouts  10.2 us (3%)
  starting transfers between devices  10 us (3%)
  other arithmetic  4.57 us (1%)
    all_gather x1, waiting for transfers between devices, dense_body(): all_tokens = lax.all_gather(tokens, AXES, axis=0, tiled=True)  134 us
    all_gather x1, blocking collectives, dense_body(): all_meta = lax.all_gather(meta, AXES, axis=0, tiled=True)  68 us
    all_gather x1, waiting for transfers between devices, dense_body(): all_grads = lax.all_gather(grad_out, AXES, axis=0, tiled=True)  41.3 us
    all_to_all x1, waiting for transfers between devices, dense_body(): lax.all_to_all(slot_grad, AXES, split_axis=0, concat_axis=0, tiled=True)  21.5 us
    dot_general x2, matrix products, rows_of(): lax.dot_general(pick, x, (((2,), (1,)), ((0,), (0,))), preferred_element_...  21.2 us
    dot_general x1, matrix products, dense_body(): lax.dot_general(grad_rows, weight_down[0], OVER_FEATURES, preferred_eleme...  11.7 us
    unnamed x33, local copies, waits for them, and re-layouts  9.29 us
  transfers between devices with their start and end apart: 4, of which 3 were waited for; matrix products, arithmetic and copies ran while one was open for 22% of the time, Pallas kernels for 0%

commit v1 on v0

--- a/solution.py
+++ b/solution.py
@@ -135,9 +135,12 @@
     capacity = saved_gate.shape[1]
     pair = capacity // experts
     f32, bf16 = (jnp.float32, jnp.bfloat16)
-    all_grads = lax.all_gather(grad_out, AXES, axis=0, tiled=True)
     meta = jnp.concatenate([expert_ids.astype(bf16), pair_slot.astype(bf16), gate_weights], axis=1)
-    all_meta = lax.all_gather(meta, AXES, axis=0, tiled=True)
+    all_grads, all_meta = jnp.split(
+        lax.all_gather(jnp.concatenate([grad_out, meta], axis=1), AXES, axis=0, tiled=True),
+        [grad_out.shape[1]],
+        axis=1,
+    )
     route = expert_ids.shape[1]
     all_meta = all_meta.reshape(experts, tok_rows, 3, route).astype(f32)
     mine = all_meta[:, :, 0] == me.astype(f32)

time: 378 us -> 395 us (1.045)
  blocking collectives: 68 us -> 0 us
  waiting for transfers between devices: 198 us -> 239 us
  local copies, waits for them, and re-layouts: 10.2 us -> 49.2 us
    all_gather x1, waiting for transfers between devices: 134 us -> 55 us  [dense_body(): all_tokens = lax.all_gather(tokens, AXES, axis=0, tiled=True)]
    all_gather x1, waiting for transfers between devices: 41.3 us -> 112 us  [dense_body(): lax.all_gather(jnp.concatenate([grad_out, meta], axis=1), AXES, axis=0, t...]
    all_gather x1 -> x0, blocking collectives: 68 us -> none  [dense_body(): all_meta = lax.all_gather(meta, AXES, axis=0, tiled=True)]
    all_to_all x1, waiting for transfers between devices: 21.5 us -> 71.4 us  [dense_body(): lax.all_to_all(slot_grad, AXES, split_axis=0, concat_axis=0, tiled=True)]
    reshape x0 -> x1, local copies, waits for them, and re-layouts: none -> 22.6 us  [rows_of(): x = x.reshape(experts, tok_rows, width)]
    split x0 -> x1, local copies, waits for them, and re-layouts: none -> 14.1 us  [dense_body(): jnp.split(lax.all_gather(jnp.concatenate([grad_out, meta], axis=1), AXES,...]
    unnamed x33 -> x29, local copies, waits for them, and re-layouts: 9.29 us -> 11.5 us
  transfers between devices with their start and end apart: 4 -> 4, of which waited for: 3 -> 3; matrix products, arithmetic and copies ran while one was open for 22% -> 30% of each run, Pallas kernels for 0% -> 0%
where the time goes in v1:
time: 395 us; the launch traced here: 394 us
  waiting for transfers between devices  239 us (61%)
  matrix products  72.2 us (18%)
  local copies, waits for them, and re-layouts  49.2 us (12%)
  between operations  14.2 us (4%)
  starting transfers between devices  11.8 us (3%)
  other arithmetic  8.09 us (2%)
    all_gather x1, waiting for transfers between devices, dense_body(): lax.all_gather(jnp.concatenate([grad_out, meta], axis=1), AXES, axis=0, t...  112 us
    all_to_all x1, waiting for transfers between devices, dense_body(): lax.all_to_all(slot_grad, AXES, split_axis=0, concat_axis=0, tiled=True)  71.4 us
    all_gather x1, waiting for transfers between devices, dense_body(): all_tokens = lax.all_gather(tokens, AXES, axis=0, tiled=True)  55 us
    reshape x1, local copies, waits for them, and re-layouts, rows_of(): x = x.reshape(experts, tok_rows, width)  22.6 us
    dot_general x2, matrix products, rows_of(): lax.dot_general(pick, x, (((2,), (1,)), ((0,), (0,))), preferred_element_...  21.1 us
    split x1, local copies, waits for them, and re-layouts, dense_body(): jnp.split(lax.all_gather(jnp.concatenate([grad_out, meta], axis=1), AXES,...  14.1 us
    dot_general x1, matrix products, dense_body(): lax.dot_general(grad_rows, weight_down[0], OVER_FEATURES, preferred_eleme...  11.8 us
    unnamed x29, local copies, waits for them, and re-layouts  11.5 us
  transfers between devices with their start and end apart: 4, of which 3 were waited for; matrix products, arithmetic and copies ran while one was open for 30% of the time, Pallas kernels for 0%

profile of v1, /device:TPU:8, one launch (start us, length us, event | category | flops | bytes accessed | tf_op | source)
XLA Modules:
  0.0 394.4 jit_solution(6413013959238108885)
XLA Ops:
  7.2 0.0 copy-start
  7.2 0.0 all-gather.3.cloned.1.call-start
  7.2 2.2 copy.46
  9.4 0.8 fusion.35
  10.2 1.9 pad_maximum_fusion
  12.1 0.0 all-gather.3.cloned.1.call-update
  12.1 0.0 all-gather.5.cloned.1.call-start
  12.2 0.7 all-gather.5.cloned.1.call-update
  12.9 4.3 %copy.48 = bf16[1,1536,768]{1,2,0:T(8,128)(2,1)} copy(bf16[1,1536,768]{2,1,0:T(8,128)(2,1)} %param.19) | data formatting | bytes 4718592 | tf_op args[9]
  17.1 4.3 %copy.49 = bf16[1,1536,768]{1,2,0:T(8,128)(2,1)} copy(bf16[1,1536,768]{2,1,0:T(8,128)(2,1)} %param.18) | data formatting | bytes 4718592 | tf_op args[8]
  21.4 111.8 %all-gather.3.cloned.1.call-done = bf16[4096,2072]{0,1:T(8,128)(2,1)} async-done(((bf16[128,2072]{0,1:T(8,128)(2,1)}), bf16[4096,2072]{0,1:T(8,128)(2,1)}) %all-gather.3.cloned.1.call-update) | async-done | bytes 16973840 | tf_op jit(solution)/shard_map/all_gather | solution.py:140
  133.2 1.0 convert_bitcast_fusion.2
  134.2 0.1 copy.55
  134.3 0.3 select_reduce_fusion.1
  134.6 0.1 mul.61
  134.7 14.1 %split.9 = bf16[4096,2048]{0,1:T(8,128)(2,1)} slice(bf16[4096,2072]{0,1:T(8,128)(2,1)} %all-gather.3.cloned.1.call-done), slice={[0:4096], [0:2048]} | slice | bytes 33554432 | tf_op jit(solution)/shard_map/split | solution.py:139
  148.8 22.6 %copy.52 = bf16[4096,2048]{1,0:T(8,128)(2,1)} copy(bf16[4096,2048]{0,1:T(8,128)(2,1)} %split.9) | data formatting | bytes 33554432 | tf_op jit(solution)/shard_map/reshape | solution.py:154
  171.4 12.8 %multiply_convert_fusion = (bf16[32,48,2048]{2,1,0:T(8,128)(2,1)}, bf16[32,48,2048]{2,1,0:T(8,128)(2,1)}) fusion(f32[32,48]{1,0:T(8,128)S(1)} %select_reduce_fusion.1, bf16[32,128,2048]{2,1,0:T(8,128)(2,1)} %bitcast.89, f32[32,128]{1,0:T(8,128)S(1)} %broadcast_add_fusion), kind=kOutput, calls=%fused_computation | convolution fusion | flops 818085888 | bytes 29382656 | tf_op jit(solution)/shard_map/dot_general | solution.py:155
  184.2 0.0 copy-done.2
  184.2 0.0 copy-done.4
  184.2 11.8 %fusion.10 = (bf16[1536]{0:T(1024)(128)(2,1)S(1)}, bf16[1536,768]{0,1:T(8,128)(2,1)}, bf16[1536,768]{0,1:T(8,128)(2,1)}) fusion(bf16[1,1536,768]{1,2,0:T(8,128)(2,1)S(1)} %copy-done.2, bf16[1,1536,768]{1,2,0:T(8,128)(2,1)S(1)} %copy-done.4, f32[1536]{0:T(1024)S(1)} %mul.61, bf16[1536,2048]{1,0:T(8,128)(2,1)} %bitcast.94, bf16[1,768,2048]{2,1,0:T(8,128)(2,1)} %param.17), kind=kOutput, calls=%fused_computation.19 | convolution fusion | flops 4854249984 | bytes 18883584 | tf_op jit(solution)/shard_map/dot_general | solution.py:165
  196.0 0.7 convert_element_type.134
  196.7 5.8 %all-to-all-start.1 = ((bf16[32,48,1]{1,2,0:T(2,128)(2,1)}), bf16[32,48,1]{1,2,0:T(2,128)(2,1)S(1)}, u32[]{:S(2)}, u32[]{:S(2)}) async-start(bf16[32,48,1]{1,2,0:T(2,128)(2,1)} %convert_element_type.134), calls=%async_computation.1 | async-start | bytes 32768 | tf_op jit(solution)/shard_map/all_to_all | solution.py:177
  202.5 0.0 copy-done
  202.5 0.0 copy-start.6
  202.5 0.0 copy-start.8
  202.5 7.1 %fusion.20 = f32[1536,2048]{1,0:T(8,128)S(1)} fusion(bf16[1536,768]{0,1:T(8,128)(2,1)} %get-tuple-element.18, bf16[1,2048,768]{2,1,0:T(8,128)(2,1)S(1)} %copy-done), kind=kOutput, calls=%fused_computation.35 | convolution fusion | flops 4831838208 | bytes 18087936 | tf_op jit(solution)/shard_map/dot_general | solution.py:173
  209.6 0.0 copy-done.6
  209.6 0.0 copy-done.8
  209.6 7.5 %add_convert_fusion = bf16[1536,2048]{1,0:T(8,128)(2,1)} fusion(f32[1536,2048]{1,0:T(8,128)S(1)} %fusion.20, bf16[1536,768]{0,1:T(8,128)(2,1)S(1)} %copy-done.8, bf16[1,2048,768]{2,1,0:T(8,128)(2,1)S(1)} %copy-done.6), kind=kOutput, calls=%fused_computation.1 | convolution fusion | flops 4838129664 | bytes 24379392 | tf_op jit(solution)/shard_map/dot_general | solution.py:174
  217.1 0.0 all-to-all-done.1
  217.1 5.9 %all-to-all-start = ((bf16[32,48,2048]{2,1,0:T(8,128)(2,1)}), bf16[32,48,2048]{2,1,0:T(8,128)(2,1)}, u32[]{:S(2)}, u32[]{:S(2)}) async-start(bf16[32,48,2048]{2,1,0:T(8,128)(2,1)} %bitcast.97), calls=%async_computation | async-start | bytes 12582912 | tf_op jit(solution)/shard_map/all_to_all | solution.py:176
  223.0 0.1 copy.45
  223.1 3.1 fusion.3
  226.3 55.0 %all-gather.5.cloned.1.call-done = bf16[4096,2048]{1,0:T(8,128)(2,1)} async-done(((bf16[128,2048]{1,0:T(8,128)(2,1)}), bf16[4096,2048]{1,0:T(8,128)(2,1)}) %all-gather.5.cloned.1.call-update) | async-done | bytes 16777232 | tf_op jit(solution)/shard_map/all_gather | solution.py:159
  281.3 8.2 %convolution_convert_fusion = bf16[32,48,2048]{2,1,0:T(8,128)(2,1)S(1)} fusion(bf16[32,128,2048]{2,1,0:T(8,128)(2,1)} %bitcast.90, f32[32,128]{1,0:T(8,128)S(1)} %broadcast_add_fusion), kind=kOutput, calls=%fused_computation.29 | convolution fusion | flops 808648704 | bytes 23085056 | tf_op jit(solution)/shard_map/dot_general | solution.py:155
  289.5 0.0 copy-done.7
  289.5 0.0 slice-start
  289.5 6.5 %fusion.24 = bf16[1,2048,768]{2,1,0:T(8,128)(2,1)} fusion(bf16[1536,2048]{1,0:T(8,128)(2,1)S(1)} %bitcast.95, bf16[1536,768]{0,1:T(8,128)(2,1)S(1)} %copy-done.7), kind=kOutput, calls=%fused_computation.39 | convolution fusion | flops 4833411072 | bytes 11796480 | tf_op jit(solution)/shard_map/dot_general | solution.py:181
  296.1 6.5 %fusion.25 = bf16[1,2048,768]{2,1,0:T(8,128)(2,1)} fusion(bf16[1536,2048]{1,0:T(8,128)(2,1)S(1)} %bitcast.96, bf16[1536,768]{0,1:T(8,128)(2,1)S(1)} %copy-done.9), kind=kOutput, calls=%fused_computation.40 | convolution fusion | flops 4833411072 | bytes 11796480 | tf_op jit(solution)/shard_map/dot_general | solution.py:182
  302.6 0.0 copy-start.1
  302.7 7.2 %fusion.26 = bf16[1,768,2048]{2,1,0:T(8,128)(2,1)} fusion(bf16[1536,2048]{1,0:T(8,128)(2,1)S(1)} %bitcast.93, bf16[1,1536,768]{1,2,0:T(8,128)(2,1)S(1)} %copy-done.3, bf16[1,1536,768]{1,2,0:T(8,128)(2,1)S(1)} %copy-done.5), kind=kOutput, calls=%fused_computation.41 | convolution fusion | flops 4842848256 | bytes 14155776 | tf_op jit(solution)/shard_map/dot_general | solution.py:179
  309.8 0.1 convert_reduce_fusion
  309.9 0.1 reshape.75
  310.0 1.0 select_reduce_fusion
  310.9 0.7 copy.51
  311.6 71.4 %all-to-all-done = bf16[32,48,2048]{2,1,0:T(8,128)(2,1)} async-done(((bf16[32,48,2048]{2,1,0:T(8,128)(2,1)}), bf16[32,48,2048]{2,1,0:T(8,128)(2,1)}, u32[]{:S(2)}, u32[]{:S(2)}) %all-to-all-start) | async-done | bytes 6291488 | tf_op jit(solution)/shard_map/all_to_all | solution.py:176
  382.9 4.6 %convolution_convert_fusion.5 = bf16[128,2048]{1,0:T(8,128)(2,1)} fusion(pred[128,1536]{1,0:T(8,128)(4,1)S(1)} %fusion.3, bf16[1536,2048]{1,0:T(8,128)(2,1)} %bitcast.8), kind=kOutput, calls=%fused_computation.42 | convolution fusion | flops 805568512 | bytes 7012352 | tf_op jit(solution)/shard_map/dot_general | solution.py:186
  (16 shorter events, 0.1 us)
Async XLA Ops:
  7.2 195.3 %copy-start = (bf16[1,2048,768]{2,1,0:T(8,128)(2,1)S(1)}, bf16[1,2048,768]{2,1,0:T(8,128)(2,1)}, u32[]{:S(2)}) copy-start(bf16[1,2048,768]{2,1,0:T(8,128)(2,1)} %param.15) | copy-start | bytes 9437188
  7.2 126.0 %all-gather.3.cloned.1.call-start = ((), (), s32[]{:S(2)}) async-start(), calls=%async_computation.2 | async-start | bytes 17504256 | tf_op jit(solution)/shard_map/all_gather | solution.py:140
  12.1 269.2 %all-gather.5.cloned.1.call-start = ((), (), s32[]{:S(2)}) async-start(), calls=%async_computation.3 | async-start | bytes 17301504 | tf_op jit(solution)/shard_map/all_gather | solution.py:159
  171.4 12.8 %copy-start.2 = (bf16[1,1536,768]{1,2,0:T(8,128)(2,1)S(1)}, bf16[1,1536,768]{1,2,0:T(8,128)(2,1)}, u32[]{:S(2)}) copy-start(bf16[1,1536,768]{1,2,0:T(8,128)(2,1)} %copy.48) | copy-start | bytes 7077892
  171.4 12.8 %copy-start.4 = (bf16[1,1536,768]{1,2,0:T(8,128)(2,1)S(1)}, bf16[1,1536,768]{1,2,0:T(8,128)(2,1)}, u32[]{:S(2)}) copy-start(bf16[1,1536,768]{1,2,0:T(8,128)(2,1)} %copy.49) | copy-start | bytes 7077892
  196.7 20.4 %all-to-all-start.1 = ((bf16[32,48,1]{1,2,0:T(2,128)(2,1)}), bf16[32,48,1]{1,2,0:T(2,128)(2,1)S(1)}, u32[]{:S(2)}, u32[]{:S(2)}) async-start(bf16[32,48,1]{1,2,0:T(2,128)(2,1)} %convert_element_type.134), calls=%async_computation.1 | async-start | bytes 32768 | tf_op jit(solution)/shard_map/all_to_all | solution.py:177
  202.5 7.1 %copy-start.6 = (bf16[1,2048,768]{2,1,0:T(8,128)(2,1)S(1)}, bf16[1,2048,768]{2,1,0:T(8,128)(2,1)}, u32[]{:S(2)}) copy-start(bf16[1,2048,768]{2,1,0:T(8,128)(2,1)} %param.16) | copy-start | bytes 9437188
  202.5 7.1 %copy-start.8 = (bf16[1536,768]{0,1:T(8,128)(2,1)S(1)}, bf16[1536,768]{0,1:T(8,128)(2,1)}, u32[]{:S(2)}) copy-start(bf16[1536,768]{0,1:T(8,128)(2,1)} %get-tuple-element.19) | copy-start | bytes 7077892
  217.1 165.8 %all-to-all-start = ((bf16[32,48,2048]{2,1,0:T(8,128)(2,1)}), bf16[32,48,2048]{2,1,0:T(8,128)(2,1)}, u32[]{:S(2)}, u32[]{:S(2)}) async-start(bf16[32,48,2048]{2,1,0:T(8,128)(2,1)} %bitcast.97), calls=%async_computation | async-start | bytes 12582912 | tf_op jit(solution)/shard_map/all_to_all | solution.py:176
  281.3 8.2 %copy-start.7 = (bf16[1536,768]{0,1:T(8,128)(2,1)S(1)}, bf16[1536,768]{0,1:T(8,128)(2,1)}, u32[]{:S(2)}) copy-start(bf16[1536,768]{0,1:T(8,128)(2,1)} %get-tuple-element.18) | copy-start | bytes 7077892
  289.5 6.6 %copy-start.9 = (bf16[1536,768]{0,1:T(8,128)(2,1)S(1)}, bf16[1536,768]{0,1:T(8,128)(2,1)}, u32[]{:S(2)}) copy-start(bf16[1536,768]{0,1:T(8,128)(2,1)} %get-tuple-element.19) | copy-start | bytes 7077892
  289.5 13.1 %slice-start = ((s8[6291456]{0:T(1024)(128)(4,1)}), s8[4194304]{0:T(1024)(128)(4,1)S(1)}, s32[]{:S(2)}) async-start(s8[6291456]{0:T(1024)(128)(4,1)} %bitcast.91), calls=%async_computation.4 | async-start | bytes 8388608
  296.1 6.5 %slice-start.1 = ((s8[6291456]{0:T(1024)(128)(4,1)}), s8[2097152]{0:T(1024)(128)(4,1)S(1)}, s32[]{:S(2)}) async-start(s8[6291456]{0:T(1024)(128)(4,1)} %bitcast.91), calls=%async_computation.5 | async-start | bytes 4194304
  296.1 6.5 %copy-start.3 = (bf16[1,1536,768]{1,2,0:T(8,128)(2,1)S(1)}, bf16[1,1536,768]{1,2,0:T(8,128)(2,1)}, u32[]{:S(2)}) copy-start(bf16[1,1536,768]{1,2,0:T(8,128)(2,1)} %copy.48) | copy-start | bytes 7077892
  296.1 6.5 %copy-start.5 = (bf16[1,1536,768]{1,2,0:T(8,128)(2,1)S(1)}, bf16[1,1536,768]{1,2,0:T(8,128)(2,1)}, u32[]{:S(2)}) copy-start(bf16[1,1536,768]{1,2,0:T(8,128)(2,1)} %copy.49) | copy-start | bytes 7077892
  302.6 84.9 %copy-start.1 = (bf16[1,2048,768]{2,1,0:T(8,128)(2,1)S(1)}, bf16[1,2048,768]{2,1,0:T(8,128)(2,1)}, u32[]{:S(2)}) copy-start(bf16[1,2048,768]{2,1,0:T(8,128)(2,1)} %param.15) | copy-start | bytes 9437188
Sparse Core Ops, SparseCore 0:
  12.2 120.9 all-gather.2
  136.2 145.0 all-gather.4
